TPU v7x, 256 devices: a whole 4x4x8 slice. The times are simulated.
256 devices in a mesh: dp: 16 (over z_hi, y, core), expert: 16 (over x, z_lo).
Axes of the slice: x: 4, y: 4, z: 8 (z_hi: 2, z_lo: 4; z = z_hi * 4 + z_lo), core: 2. Of those that a mesh axis runs over, the one named last changes fastest.
Arguments:
- images: bfloat16 [1024, 256, 1280], P(('dp', 'expert')), may hold values from -16 to 16
- router: bfloat16 [1280, 128], replicated, as said below
- w_in: bfloat16 [256, 1280, 1280], P(('dp', 'expert')), may hold values from -0.15625 to 0.15625
- w_out: bfloat16 [256, 1280, 1280], P(('dp', 'expert')), may hold values from -0.125 to 0.125
- keep_bits: int32 [1024, 256, 128], P(None, ('dp', 'expert')), may hold values from 0 to 1023, as said below
Outputs:
- mixed: bfloat16 [1024, 256, 1280], P(('dp', 'expert'))
Inputs may be any that keep to these rules, and one draw needn't show every extreme that they name: `router`: each entry within 18 / sqrt(1280) in magnitude. `keep_bits`: bit i of word w stands for hidden unit 10 * w + i.
All inputs are finite; a program needn't handle non-finite values.
Results may differ from a plain program's by a relative error of at most 0.017.
Values may be sent and summed in bfloat16 or wider, within the bound.
A program may use at most 128 MiB of HBM per device.

v0:
```python
import jax
import jax.numpy as jnp
from jax import lax
from jax.sharding import PartitionSpec as P

SPLIT = 2
keep_rate = 0.875


def unpack_flags(words):
    shifts = jnp.arange(10, dtype=jnp.int32)
    flags = jnp.right_shift(words[..., None], shifts) & 1
    return flags.reshape(words.shape[:-1] + (words.shape[-1] * 10,)).astype(jnp.float32)


def expert_piece(slot_rows, w_in, w_out, kept_units):
    pre_act = jnp.dot(slot_rows, w_in[0], preferred_element_type=jnp.float32)
    hidden = (jax.nn.gelu(pre_act) * kept_units * (1.0 / keep_rate)).astype(jnp.bfloat16)
    return jnp.dot(hidden, w_out[0], preferred_element_type=jnp.float32).astype(jnp.bfloat16)


def on_device(images, router, w_in, w_out, keep_bits):
    image_count = images.shape[0]
    width = images.shape[2]
    experts = router.shape[1]
    dp_count = lax.axis_size("dp")
    expert_count = lax.axis_size("expert")
    logits = jnp.einsum("bmd,de->bme", images, router, preferred_element_type=jnp.float32)
    dispatch = jax.nn.softmax(logits, axis=1).astype(jnp.bfloat16)
    combine = jax.nn.softmax(logits, axis=2).astype(jnp.bfloat16)
    slot_values = jnp.einsum(
        "bme,bmd->bed", dispatch, images, preferred_element_type=jnp.float32
    ).astype(jnp.bfloat16)
    kept_units = unpack_flags(keep_bits[:, 0, :])
    doubled = jnp.repeat(slot_values, SPLIT, axis=1).reshape(
        image_count, dp_count, expert_count, width
    )
    across = lax.all_to_all(doubled, "expert", split_axis=2, concat_axis=0, tiled=True)
    arrived = lax.all_to_all(across, "dp", split_axis=1, concat_axis=0, tiled=True)
    partial_value = expert_piece(arrived.reshape(-1, width), w_in, w_out, kept_units)
    returned = lax.all_to_all(
        partial_value.reshape(-1, 1, 1, width), "dp", split_axis=0, concat_axis=1, tiled=True
    )
    returned = lax.all_to_all(returned, "expert", split_axis=0, concat_axis=2, tiled=True)
    paired = returned.reshape(image_count, experts, SPLIT, width)
    expert_out = paired.astype(jnp.float32).sum(axis=2).astype(jnp.bfloat16)
    mixed = jnp.einsum("bme,bed->bmd", combine, expert_out, preferred_element_type=jnp.float32)
    return mixed.astype(jnp.bfloat16)


def solution(mesh):
    placed = (
        P(("dp", "expert"), None, None),
        P(),
        P(("dp", "expert"), None, None),
        P(("dp", "expert"), None, None),
        P(None, ("dp", "expert"), None),
    )
    return jax.shard_map(
        on_device,
        mesh=mesh,
        in_specs=placed,
        out_specs=P(("dp", "expert"), None, None),
        check_vma=False,
    )
```

profile of v0, /device:TPU:1, one launch (start us, length us, event | category | flops | bytes accessed | tf_op | source)
XLA Modules:
  0.0 342.5 jit_solution(12739725940960338433)
XLA Ops:
  0.0 0.0 copy-start
  0.0 2.7 fusion.27
  2.8 0.0 copy-start.2
  2.8 0.8 copy-done.2
  3.6 0.1 fusion.39
  3.7 3.7 %convolution_convert_fusion.2 = bf16[4,128,1280]{2,1,0:T(8,128)(2,1)} fusion(bf16[4,256,1280]{2,1,0:T(8,128)(2,1)} %param.5, f32[4,128]{1,0:T(4,128)S(1)} %fusion.39, f32[4,256,128]{2,1,0:T(8,128)} %copy-done.2), kind=kOutput, calls=%fused_computation.19 | convolution fusion | flops 336593664 | bytes 4458496 | tf_op jit(solution)/shard_map/bme,bmd->bed/dot_general | solution.py:31
  7.4 2.3 copy.31
  9.8 0.7 broadcast_in_dim.2
  10.5 1.2 copy.32
  11.7 69.5 %all_to_all.66 = bf16[4,16,16,1280]{3,0,1,2:T(4,128)(2,1)S(1)} all-to-all(bf16[4,16,16,1280]{3,0,1,2:T(4,128)(2,1)S(1)} %copy.32), channel_id=1, replica_groups=mesh['dp'=16,'expert'=16] {'expert'}, dimensions={2} | all-to-all | bytes 5242880 | tf_op jit(solution)/shard_map/all_to_all | solution.py:38
  81.2 0.4 copy.33
  81.6 2.3 copy.34
  83.9 10.1 %all-to-all-start.1 = ((bf16[64,16,1,1280]{3,0,2,1:T(8,128)(2,1)}), bf16[64,16,1,1280]{3,0,2,1:T(8,128)(2,1)}, u32[]{:S(2)}, u32[]{:S(2)}) async-start(bf16[64,16,1,1280]{3,0,2,1:T(8,128)(2,1)} %copy.34), calls=%async_computation.1 | async-start | bytes 5242880 | tf_op jit(solution)/shard_map/all_to_all | solution.py:39
  94.0 2.1 copy.37
  96.1 5.4 %shift_right_arithmetic.23 = s32[1024,128,10]{0,2,1:T(8,128)} broadcast(s32[1024,128]{0,1:T(8,128)} %copy.37), dimensions={0,1} | broadcast | bytes 5767168 | tf_op jit(solution)/shard_map/shift_right_arithmetic | solution.py:12
  101.5 7.9 %shift_right_arithmetic.24 = s32[1024,1280]{0,1:T(8,128)} reshape(s32[1024,128,10]{0,2,1:T(8,128)} %shift_right_arithmetic.23) | data formatting | bytes 10485760 | tf_op jit(solution)/shard_map/shift_right_arithmetic | solution.py:12
  109.4 5.9 %copy.38 = s32[1024,1280]{1,0:T(8,128)} copy(s32[1024,1280]{0,1:T(8,128)} %shift_right_arithmetic.24) | data formatting | bytes 10485760 | tf_op jit(solution)/shard_map/shift_right_arithmetic | solution.py:12
  115.3 0.1 shift_right_arithmetic.26
  115.5 41.3 %all-to-all-done.1 = bf16[64,16,1,1280]{3,0,2,1:T(8,128)(2,1)} async-done(((bf16[64,16,1,1280]{3,0,2,1:T(8,128)(2,1)}), bf16[64,16,1,1280]{3,0,2,1:T(8,128)(2,1)}, u32[]{:S(2)}, u32[]{:S(2)}) %all-to-all-start.1) | async-done | bytes 2621472 | tf_op jit(solution)/shard_map/all_to_all | solution.py:39
  156.8 3.2 copy.48
  159.9 2.3 copy.36
  162.2 0.0 copy-done
  162.2 11.8 %fusion.17 = bf16[1024,1,1,1280]{3,0,2,1:T(8,128)(2,1)} fusion(bf16[1,1280,1280]{2,1,0:T(8,128)(2,1)S(1)} %copy-done, s32[1024,1280]{1,0:T(8,128)} %copy.38, bf16[1024,1280]{1,0:T(8,128)(2,1)} %bitcast.54, bf16[1,1280,1280]{2,1,0:T(8,128)(2,1)} %param.7, s32[1280]{0:T(1024)S(1)} %shift_right_arithmetic.26), kind=kOutput, calls=%fused_computation.18 | convolution fusion | flops 6730547200 | bytes 17044480 | tf_op jit(solution)/shard_map/dot_general | solution.py:19
  174.0 0.5 broadcast.8
  174.6 4.5 %reduce.1 = bf16[1024,1280]{1,0:T(8,128)(2,1)S(1)} reduce(bf16[1024,1,1,1280]{3,0,2,1:T(8,128)(2,1)} %fusion.17, bf16[]{:T(256)} %broadcast.8), dimensions={1,2}, to_apply=%copy.39.reduce_sub_computation | reduce | bytes 5242882 | tf_op jit(solution)/shard_map/reshape | solution.py:42
  179.0 2.2 reshape.23
  181.2 57.8 %all_to_all.67 = bf16[16,2,40960]{2,1,0:T(2,128)(2,1)S(1)} all-to-all(bf16[16,2,40960]{2,1,0:T(2,128)(2,1)} %reshape.23), channel_id=1, replica_groups=mesh['dp'=16,'expert'=16] {'dp'}, dimensions={0} | all-to-all | bytes 5242880 | tf_op jit(solution)/shard_map/all_to_all | solution.py:41
  239.0 7.2 %reshape.24 = bf16[1024,1,1,1280]{3,2,1,0:T(2,128)(2,1)} reshape(bf16[16,2,40960]{2,1,0:T(2,128)(2,1)S(1)} %all_to_all.67) | data formatting | bytes 5242880
  246.2 2.9 copy.44
  249.1 2.9 copy.40
  252.0 0.0 copy-start.3
  252.0 15.0 %all-to-all-start.3 = ((bf16[64,16,1,1280]{3,1,2,0:T(8,128)(2,1)}), bf16[64,16,1,1280]{3,1,2,0:T(8,128)(2,1)S(1)}, u32[]{:S(2)}, u32[]{:S(2)}) async-start(bf16[64,16,1,1280]{3,1,2,0:T(8,128)(2,1)} %copy.40), calls=%async_computation.3 | async-start | bytes 5242880 | tf_op jit(solution)/shard_map/all_to_all | solution.py:44
  267.0 0.0 copy-done.3
  267.0 0.4 fusion.40
  267.4 61.9 %all-to-all-done.3 = bf16[64,16,1,1280]{3,1,2,0:T(8,128)(2,1)S(1)} async-done(((bf16[64,16,1,1280]{3,1,2,0:T(8,128)(2,1)}), bf16[64,16,1,1280]{3,1,2,0:T(8,128)(2,1)S(1)}, u32[]{:S(2)}, u32[]{:S(2)}) %all-to-all-start.3) | async-done | bytes 2621472 | tf_op jit(solution)/shard_map/all_to_all | solution.py:44
  329.3 2.8 copy.41
  332.1 0.0 copy-start.1
  332.1 5.1 %reduce_sum.32 = bf16[4,128,1280]{2,0,1:T(4,128)(2,1)} reduce(bf16[4,128,2,1280]{3,0,2,1:T(4,128)(2,1)} %bitcast.49, bf16[]{:T(256)} %constant.8.clone.1), dimensions={2}, to_apply=%region_4.0 | reduce | flops 655360 | bytes 3932162 | tf_op jit(solution)/shard_map/reduce_sum | solution.py:46
  337.2 5.3 %convolution_convert_fusion = bf16[4,256,1280]{2,1,0:T(8,128)(2,1)} fusion(bf16[4,128,1280]{2,0,1:T(4,128)(2,1)} %reduce_sum.32, f32[4,256]{1,0:T(4,128)S(1)} %fusion.40, f32[4,256,128]{2,1,0:T(8,128)} %copy-done.2), kind=kOutput, calls=%fused_computation.13 | convolution fusion | flops 337249408 | bytes 4460544 | tf_op jit(solution)/shard_map/bme,bed->bmd/dot_general | solution.py:47
  342.5 0.0 copy-done.1
  (1 shorter events, 0.0 us)
Async XLA Ops:
  0.0 162.2 %copy-start = (bf16[1,1280,1280]{2,1,0:T(8,128)(2,1)S(1)}, bf16[1,1280,1280]{2,1,0:T(8,128)(2,1)}, u32[]{:S(2)}) copy-start(bf16[1,1280,1280]{2,1,0:T(8,128)(2,1)} %param.8) | copy-start | bytes 9830404
  2.8 0.8 copy-start.2
  83.9 72.9 %all-to-all-start.1 = ((bf16[64,16,1,1280]{3,0,2,1:T(8,128)(2,1)}), bf16[64,16,1,1280]{3,0,2,1:T(8,128)(2,1)}, u32[]{:S(2)}, u32[]{:S(2)}) async-start(bf16[64,16,1,1280]{3,0,2,1:T(8,128)(2,1)} %copy.34), calls=%async_computation.1 | async-start | bytes 5242880 | tf_op jit(solution)/shard_map/all_to_all | solution.py:39
  252.0 15.0 %copy-start.3 = (f32[4,256,128]{2,1,0:T(8,128)S(1)}, f32[4,256,128]{2,1,0:T(8,128)}, u32[]{:S(2)}) copy-start(f32[4,256,128]{2,1,0:T(8,128)} %copy-done.2) | copy-start | bytes 1572868
  252.0 77.2 %all-to-all-start.3 = ((bf16[64,16,1,1280]{3,1,2,0:T(8,128)(2,1)}), bf16[64,16,1,1280]{3,1,2,0:T(8,128)(2,1)S(1)}, u32[]{:S(2)}, u32[]{:S(2)}) async-start(bf16[64,16,1,1280]{3,1,2,0:T(8,128)(2,1)} %copy.40), calls=%async_computation.3 | async-start | bytes 5242880 | tf_op jit(solution)/shard_map/all_to_all | solution.py:44
  332.1 10.4 %copy-start.1 = (bf16[1,1280,1280]{2,1,0:T(8,128)(2,1)S(1)}, bf16[1,1280,1280]{2,1,0:T(8,128)(2,1)}, u32[]{:S(2)}) copy-start(bf16[1,1280,1280]{2,1,0:T(8,128)(2,1)} %param.8) | copy-start | bytes 9830404
where the time goes:
time: 343 us; the launch traced here: 342 us
  blocking collectives  127 us (37%)
  waiting for transfers between devices  103 us (30%)
  local copies, waits for them, and re-layouts  53.2 us (16%)
  starting transfers between devices  25.1 us (7%)
  matrix products  23.6 us (7%)
  other arithmetic  10.1 us (3%)
    all_to_all x1, blocking collectives, on_device(): lax.all_to_all(doubled, 'expert', split_axis=2, concat_axis=0, tiled=True)  69.5 us
    all_to_all x1, waiting for transfers between devices, on_device(): lax.all_to_all(returned, 'expert', split_axis=0, concat_axis=2, tiled=True)  61.9 us
    all_to_all x1, blocking collectives, on_device(): lax.all_to_all(partial_value.reshape(-1, 1, 1, width), 'dp', split_axis=0...  57.8 us
    all_to_all x1, waiting for transfers between devices, on_device(): lax.all_to_all(across, 'dp', split_axis=1, concat_axis=0, tiled=True)  41.3 us
    shift_right_arithmetic x6, local copies, waits for them, and re-layouts, unpack_flags(): flags = jnp.right_shift(words[..., None], shifts) & 1  21.5 us
    all_to_all x1, starting transfers between devices, on_device(): lax.all_to_all(returned, 'expert', split_axis=0, concat_axis=2, tiled=True)  15 us
    unnamed x11, local copies, waits for them, and re-layouts  13.1 us
    dot_general x1, matrix products, expert_piece(): jnp.dot(hidden, w_out[0], preferred_element_type=jnp.float32)  11.8 us
  transfers between devices with their start and end apart: 2, of which 2 were waited for; matrix products, arithmetic and copies ran while one was open for 6% of the time, Pallas kernels for 0%

commit v1 on v0

--- a/solution.py
+++ b/solution.py
@@ -36,7 +36,11 @@
         image_count, dp_count, expert_count, width
     )
     across = lax.all_to_all(doubled, "expert", split_axis=2, concat_axis=0, tiled=True)
-    arrived = lax.all_to_all(across, "dp", split_axis=1, concat_axis=0, tiled=True)
+    time_points_on_mesh = lambda q_in, dim_at, dim_no: jnp.concatenate(
+        lax.all_to_all(jnp.stack(jnp.split(q_in, lax.axis_size("dp"), axis=dim_at)), "dp", 0, 0),
+        axis=dim_no,
+    )
+    arrived = time_points_on_mesh(across, 1, 0)
     partial_value = expert_piece(arrived.reshape(-1, width), w_in, w_out, kept_units)
     returned = lax.all_to_all(
         partial_value.reshape(-1, 1, 1, width), "dp", split_axis=0, concat_axis=1, tiled=True

time: 343 us -> 352 us (1.026)
  local copies, waits for them, and re-layouts: 53.2 us -> 62.2 us
    unnamed x11 -> x26, local copies, waits for them, and re-layouts: 13.1 us -> 23.4 us
    split x0 -> x1, local copies, waits for them, and re-layouts: none -> 5.71 us  [on_device(): jnp.split(q_in, lax.axis_size('dp'), axis=dim_at)]
    all_to_all x2 -> x0, local copies, waits for them, and re-layouts: 5.45 us -> none  [on_device(): lax.all_to_all(across, 'dp', split_axis=1, concat_axis=0, tiled=True)]
where the time goes in v1:
time: 352 us
  blocking collectives  127 us (36%)
  waiting for transfers between devices  103 us (29%)
  local copies, waits for them, and re-layouts  62.2 us (18%)
  starting transfers between devices  25.1 us (7%)
  matrix products  23.6 us (7%)
  other arithmetic  10.1 us (3%)
    all_to_all x1, blocking collectives, on_device(): lax.all_to_all(doubled, 'expert', split_axis=2, concat_axis=0, tiled=True)  69.5 us
    all_to_all x1, waiting for transfers between devices, on_device(): lax.all_to_all(returned, 'expert', split_axis=0, concat_axis=2, tiled=True)  61.9 us
    all_to_all x1, blocking collectives, on_device(): lax.all_to_all(partial_value.reshape(-1, 1, 1, width), 'dp', split_axis=0...  57.8 us
    all_to_all x1, waiting for transfers between devices, on_device(): lax.all_to_all(jnp.stack(jnp.split(q_in, lax.axis_size('dp'), axis=dim_at...  41.3 us
    unnamed x26, local copies, waits for them, and re-layouts  23.4 us
    shift_right_arithmetic x6, local copies, waits for them, and re-layouts, unpack_flags(): flags = jnp.right_shift(words[..., None], shifts) & 1  21.5 us
    all_to_all x1, starting transfers between devices, on_device(): lax.all_to_all(returned, 'expert', split_axis=0, concat_axis=2, tiled=True)  15 us
    dot_general x1, matrix products, expert_piece(): jnp.dot(hidden, w_out[0], preferred_element_type=jnp.float32)  11.8 us
  transfers between devices with their start and end apart: 2, of which 2 were waited for; matrix products, arithmetic and copies ran while one was open for 6% of the time, Pallas kernels for 0%

profile of v1, /device:TPU:1, one launch (start us, length us, event | category | flops | bytes accessed | tf_op | source)
XLA Modules:
  0.0 351.6 jit_solution(3386568633561916066)
XLA Ops:
  0.0 0.0 copy-start
  0.0 2.7 fusion.27
  2.8 0.0 copy-start.2
  2.8 0.8 copy-done.2
  3.6 0.1 fusion.40
  3.7 3.7 %convolution_convert_fusion.2 = bf16[4,128,1280]{2,1,0:T(8,128)(2,1)} fusion(bf16[4,256,1280]{2,1,0:T(8,128)(2,1)} %param.5, f32[4,128]{1,0:T(4,128)S(1)} %fusion.40, f32[4,256,128]{2,1,0:T(8,128)} %copy-done.2), kind=kOutput, calls=%fused_computation.19 | convolution fusion | flops 336593664 | bytes 4458496 | tf_op jit(solution)/shard_map/bme,bmd->bed/dot_general | solution.py:31
  7.4 2.3 copy.216
  9.8 0.7 broadcast_in_dim.2
  10.5 1.2 copy.217
  11.7 69.5 %all_to_all.56 = bf16[4,16,16,1280]{3,0,1,2:T(4,128)(2,1)S(1)} all-to-all(bf16[4,16,16,1280]{3,0,1,2:T(4,128)(2,1)S(1)} %copy.217), channel_id=1, replica_groups=mesh['dp'=16,'expert'=16] {'expert'}, dimensions={2} | all-to-all | bytes 5242880 | tf_op jit(solution)/shard_map/all_to_all | solution.py:38
  81.2 0.4 copy.218
  81.6 5.7 %fusion.39 = (bf16[64,1,1,1280]{3,1,0,2:T(2,128)(2,1)S(1)}, bf16[64,1,1,1280]{3,1,0,2:T(2,128)(2,1)S(1)}, bf16[64,1,1,1280]{3,1,0,2:T(2,128)(2,1)S(1)}, bf16[64,...) fusion(bf16[64,16,1,1280]{3,1,0,2:T(8,128)(2,1)S(1)} %bitcast.75), kind=kLoop, calls=%fused_computation.55 | loop fusion | bytes 5242880 | tf_op jit(solution)/shard_map/split | solution.py:40
  87.3 0.7 bitcast_dynamic-update-slice_fusion.15
  88.0 0.7 bitcast_dynamic-update-slice_fusion.14
  88.7 0.7 bitcast_dynamic-update-slice_fusion.13
  89.4 0.7 bitcast_dynamic-update-slice_fusion.12
  90.1 0.7 bitcast_dynamic-update-slice_fusion.11
  90.8 0.7 bitcast_dynamic-update-slice_fusion.10
  91.5 0.7 bitcast_dynamic-update-slice_fusion.9
  92.1 0.7 bitcast_dynamic-update-slice_fusion.8
  92.8 0.7 bitcast_dynamic-update-slice_fusion.7
  93.5 0.7 bitcast_dynamic-update-slice_fusion.6
  94.2 0.7 bitcast_dynamic-update-slice_fusion.5
  94.9 0.7 bitcast_dynamic-update-slice_fusion.4
  95.6 0.7 bitcast_dynamic-update-slice_fusion.3
  96.3 0.7 bitcast_dynamic-update-slice_fusion.2
  96.9 0.7 bitcast_dynamic-update-slice_fusion.1
  97.6 0.7 bitcast_dynamic-update-slice_fusion
  98.3 10.1 %all-to-all-start.1 = ((bf16[16,64,1,1,1280]{4,1,3,2,0:T(8,128)(2,1)}), bf16[16,64,1,1,1280]{4,1,3,2,0:T(8,128)(2,1)}, u32[]{:S(2)}, u32[]{:S(2)}) async-start(bf16[16,64,1,1,1280]{4,1,3,2,0:T(8,128)(2,1)} %bitcast_dynamic-update-slice_fusion), calls=%async_computation.1 | async-start | bytes 5242880 | tf_op jit(solution)/shard_map/all_to_all | solution.py:40
  108.4 2.1 copy.219
  110.5 5.4 %shift_right_arithmetic.23 = s32[1024,128,10]{0,2,1:T(8,128)} broadcast(s32[1024,128]{0,1:T(8,128)} %copy.219), dimensions={0,1} | broadcast | bytes 5767168 | tf_op jit(solution)/shard_map/shift_right_arithmetic | solution.py:12
  115.9 7.9 %shift_right_arithmetic.24 = s32[1024,1280]{0,1:T(8,128)} reshape(s32[1024,128,10]{0,2,1:T(8,128)} %shift_right_arithmetic.23) | data formatting | bytes 10485760 | tf_op jit(solution)/shard_map/shift_right_arithmetic | solution.py:12
  123.8 5.9 %copy.220 = s32[1024,1280]{1,0:T(8,128)} copy(s32[1024,1280]{0,1:T(8,128)} %shift_right_arithmetic.24) | data formatting | bytes 10485760 | tf_op jit(solution)/shard_map/shift_right_arithmetic | solution.py:12
  129.7 0.1 shift_right_arithmetic.26
  129.9 41.3 %all-to-all-done.1 = bf16[16,64,1,1,1280]{4,1,3,2,0:T(8,128)(2,1)} async-done(((bf16[16,64,1,1,1280]{4,1,3,2,0:T(8,128)(2,1)}), bf16[16,64,1,1,1280]{4,1,3,2,0:T(8,128)(2,1)}, u32[]{:S(2)}, u32[]{:S(2)}) %all-to-all-start.1) | async-done | bytes 2621472 | tf_op jit(solution)/shard_map/all_to_all | solution.py:40
  171.2 0.0 copy-done
  171.2 11.8 %fusion.17 = bf16[1024,1,1,1280]{3,0,2,1:T(8,128)(2,1)} fusion(bf16[1,1280,1280]{2,1,0:T(8,128)(2,1)S(1)} %copy-done, s32[1024,1280]{1,0:T(8,128)} %copy.220, bf16[1024,1280]{1,0:T(8,128)(2,1)} %bitcast.7, bf16[1,1280,1280]{2,1,0:T(8,128)(2,1)} %param.7, s32[1280]{0:T(1024)S(1)} %shift_right_arithmetic.26), kind=kOutput, calls=%fused_computation.18 | convolution fusion | flops 6730547200 | bytes 17044480 | tf_op jit(solution)/shard_map/dot_general | solution.py:19
  183.0 0.6 broadcast.8
  183.6 4.5 %reduce.1 = bf16[1024,1280]{1,0:T(8,128)(2,1)S(1)} reduce(bf16[1024,1,1,1280]{3,0,2,1:T(8,128)(2,1)} %fusion.17, bf16[]{:T(256)} %broadcast.8), dimensions={1,2}, to_apply=%copy.221.reduce_sub_computation | reduce | bytes 5242882 | tf_op jit(solution)/shard_map/reshape | solution.py:46
  188.1 2.2 reshape.18
  190.3 57.8 %all_to_all.57 = bf16[16,2,40960]{2,1,0:T(2,128)(2,1)S(1)} all-to-all(bf16[16,2,40960]{2,1,0:T(2,128)(2,1)} %reshape.18), channel_id=1, replica_groups=mesh['dp'=16,'expert'=16] {'dp'}, dimensions={0} | all-to-all | bytes 5242880 | tf_op jit(solution)/shard_map/all_to_all | solution.py:45
  248.1 7.2 %reshape.19 = bf16[1024,1,1,1280]{3,2,1,0:T(2,128)(2,1)} reshape(bf16[16,2,40960]{2,1,0:T(2,128)(2,1)S(1)} %all_to_all.57) | data formatting | bytes 5242880
  255.3 2.9 copy.242
  258.2 2.9 copy.222
  261.1 0.0 copy-start.3
  261.1 15.0 %all-to-all-start.3 = ((bf16[64,16,1,1280]{3,1,2,0:T(8,128)(2,1)}), bf16[64,16,1,1280]{3,1,2,0:T(8,128)(2,1)S(1)}, u32[]{:S(2)}, u32[]{:S(2)}) async-start(bf16[64,16,1,1280]{3,1,2,0:T(8,128)(2,1)} %copy.222), calls=%async_computation.3 | async-start | bytes 5242880 | tf_op jit(solution)/shard_map/all_to_all | solution.py:48
  276.1 0.0 copy-done.3
  276.1 0.4 fusion.41
  276.5 61.9 %all-to-all-done.3 = bf16[64,16,1,1280]{3,1,2,0:T(8,128)(2,1)S(1)} async-done(((bf16[64,16,1,1280]{3,1,2,0:T(8,128)(2,1)}), bf16[64,16,1,1280]{3,1,2,0:T(8,128)(2,1)S(1)}, u32[]{:S(2)}, u32[]{:S(2)}) %all-to-all-start.3) | async-done | bytes 2621472 | tf_op jit(solution)/shard_map/all_to_all | solution.py:48
  338.3 2.8 copy.223
  341.2 0.0 copy-start.1
  341.2 5.1 %reduce_sum.32 = bf16[4,128,1280]{2,0,1:T(4,128)(2,1)} reduce(bf16[4,128,2,1280]{3,0,2,1:T(4,128)(2,1)} %bitcast.77, bf16[]{:T(256)} %constant.8.clone.1), dimensions={2}, to_apply=%region_4.0 | reduce | flops 655360 | bytes 3932162 | tf_op jit(solution)/shard_map/reduce_sum | solution.py:50
  346.3 5.3 %convolution_convert_fusion = bf16[4,256,1280]{2,1,0:T(8,128)(2,1)} fusion(bf16[4,128,1280]{2,0,1:T(4,128)(2,1)} %reduce_sum.32, f32[4,256]{1,0:T(4,128)S(1)} %fusion.41, f32[4,256,128]{2,1,0:T(8,128)} %copy-done.2), kind=kOutput, calls=%fused_computation.13 | convolution fusion | flops 337249408 | bytes 4460544 | tf_op jit(solution)/shard_map/bme,bed->bmd/dot_general | solution.py:51
  351.6 0.0 copy-done.1
  (1 shorter events, 0.0 us)
Async XLA Ops:
  0.0 171.2 %copy-start = (bf16[1,1280,1280]{2,1,0:T(8,128)(2,1)S(1)}, bf16[1,1280,1280]{2,1,0:T(8,128)(2,1)}, u32[]{:S(2)}) copy-start(bf16[1,1280,1280]{2,1,0:T(8,128)(2,1)} %param.8) | copy-start | bytes 9830404
  2.8 0.8 copy-start.2
  98.3 72.9 %all-to-all-start.1 = ((bf16[16,64,1,1,1280]{4,1,3,2,0:T(8,128)(2,1)}), bf16[16,64,1,1,1280]{4,1,3,2,0:T(8,128)(2,1)}, u32[]{:S(2)}, u32[]{:S(2)}) async-start(bf16[16,64,1,1,1280]{4,1,3,2,0:T(8,128)(2,1)} %bitcast_dynamic-update-slice_fusion), calls=%async_computation.1 | async-start | bytes 5242880 | tf_op jit(solution)/shard_map/all_to_all | solution.py:40
  261.1 15.0 %copy-start.3 = (f32[4,256,128]{2,1,0:T(8,128)S(1)}, f32[4,256,128]{2,1,0:T(8,128)}, u32[]{:S(2)}) copy-start(f32[4,256,128]{2,1,0:T(8,128)} %copy-done.2) | copy-start | bytes 1572868
  261.1 77.2 %all-to-all-start.3 = ((bf16[64,16,1,1280]{3,1,2,0:T(8,128)(2,1)}), bf16[64,16,1,1280]{3,1,2,0:T(8,128)(2,1)S(1)}, u32[]{:S(2)}, u32[]{:S(2)}) async-start(bf16[64,16,1,1280]{3,1,2,0:T(8,128)(2,1)} %copy.222), calls=%async_computation.3 | async-start | bytes 5242880 | tf_op jit(solution)/shard_map/all_to_all | solution.py:48
  341.2 10.4 %copy-start.1 = (bf16[1,1280,1280]{2,1,0:T(8,128)(2,1)S(1)}, bf16[1,1280,1280]{2,1,0:T(8,128)(2,1)}, u32[]{:S(2)}) copy-start(bf16[1,1280,1280]{2,1,0:T(8,128)(2,1)} %param.8) | copy-start | bytes 9830404
